TPU v7x, 32 devices: a whole 2x2x4 slice. The times are simulated.
32 devices in a mesh: dp: 8 (over y, x, core), ctx: 4 (over z).
Axes of the slice: x: 2, y: 2, z: 4, core: 2. Of those that a mesh axis runs over, the one named last changes fastest.
Arguments:
- hidden_in: float32 [8, 512, 960], P('dp', 'ctx'), may hold values from -6 to 6
- segments: int32 [8, 512], P('dp'), may hold values from 0 to 3, never falling along the last dimension, each value on 1 to 256 neighbouring positions
- attn_flat: bfloat16 [19200, 128], P(('dp', 'ctx')), may hold values from -6 to 6
- mlp_flat: bfloat16 [57600, 128], P(('dp', 'ctx')), may hold values from -6 to 6
- norm_one: float32 [960], replicated, may hold values from 0.1 to 1.9
- norm_two: float32 [960], replicated, may hold values from 0.1 to 1.9
- cotangent: float32 [8, 512, 960], P('dp', 'ctx'), may hold values from -6 to 6
Outputs:
- block_out: float32 [8, 512, 960], P('dp', 'ctx')
- grad_in: float32 [8, 512, 960], P('dp', 'ctx')
- attn_grad: float32 [19200, 128], P(('dp', 'ctx'))
- mlp_grad: float32 [57600, 128], P(('dp', 'ctx'))
- norm_one_grad: float32 [960], replicated
- norm_two_grad: float32 [960], replicated
Inputs may be any that keep to these rules, and one draw needn't show every extreme that they name: `segments`: segment numbers never fall along a sequence; each document covers at most 256 positions, some document exactly that many.
All inputs are finite; a program needn't handle non-finite values.
Results may differ from a plain program's by a relative error of at most 0.015.
Values may be sent and summed in bfloat16 or wider, within the bound.
No kernel may reach another device: no remote copies, remote signals or barrier semaphores. Data moves between devices by JAX's collectives and lax.ppermute only.
A program may use at most 128 MiB of HBM per device.

v0:
```python
import jax
import jax.numpy as jnp
from jax import lax
from jax.sharding import PartitionSpec as P

D = 960
HEADS = 15
KV_HEADS = 5
HEAD_DIM = 64
FFN = 2560
EPS = 1e-05
THETA = 100000.0


def positions_of(segment_ids):
    earlier = (segment_ids[..., None, :] < segment_ids[..., :, None]).astype(jnp.int32)
    total_len = segment_ids.shape[-1]
    return jnp.arange(total_len, dtype=jnp.int32) - jnp.sum(earlier, axis=-1)


def rope_tables(positions):
    half_dim = HEAD_DIM // 2
    frequency = THETA ** (-2.0 * jnp.arange(half_dim, dtype=jnp.float32) / HEAD_DIM)
    angles = positions.astype(jnp.float32)[:, None] * frequency[None, :]
    return (jnp.cos(angles)[:, None, :], jnp.sin(angles)[:, None, :])


def rotate(vectors, cosine_table, sine_table):
    half_dim = vectors.shape[-1] // 2
    lower_half = vectors[..., :half_dim]
    upper_half = vectors[..., half_dim:]
    return jnp.concatenate(
        [
            lower_half * cosine_table - upper_half * sine_table,
            upper_half * cosine_table + lower_half * sine_table,
        ],
        axis=-1,
    )


def unrotate(grad_rows, cosine_table, sine_table):
    half_dim = grad_rows.shape[-1] // 2
    lower_half = grad_rows[..., :half_dim]
    upper_half = grad_rows[..., half_dim:]
    return jnp.concatenate(
        [
            lower_half * cosine_table + upper_half * sine_table,
            upper_half * cosine_table - lower_half * sine_table,
        ],
        axis=-1,
    )


def unpack_blocks(flat_rows, shapes, dp_count, ctx_count):
    pieces = flat_rows.reshape(dp_count, ctx_count, -1).transpose(1, 0, 2).reshape(ctx_count, -1)
    matrices = []
    offset = 0
    for height, width_cols in shapes:
        length = height * width_cols // ctx_count
        matrices.append(pieces[:, offset : offset + length].reshape(height, width_cols))
        offset = offset + length
    return matrices


def norm_forward(residual, gain_vec):
    inverse = lax.rsqrt(jnp.mean(residual * residual, axis=-1, keepdims=True) + EPS)
    return (inverse, residual * inverse * gain_vec)


def norm_backward(residual, inverse, gain_vec, grad_normed):
    scaled = grad_normed * gain_vec
    cubed = inverse * inverse * inverse
    grad_resid = inverse * scaled - residual * cubed * jnp.mean(
        scaled * residual, axis=-1, keepdims=True
    )
    grad_gain = jnp.sum(grad_normed * residual * inverse, axis=0)
    return (grad_resid, grad_gain)


def masked_scores(query_rot, key_whole, allowed, score_scale):
    scores = (
        jnp.einsum("sqkgd,slkd->skgql", query_rot, key_whole, preferred_element_type=jnp.float32)
        * score_scale
    )
    return jnp.where(allowed, scores, -jnp.inf)


def left_dot(left_cols, right_rows):
    return lax.dot_general(
        left_cols, right_rows, (((0,), (0,)), ((), ())), preferred_element_type=jnp.float32
    )


def body(hidden_in, segments, attn_flat, mlp_flat, norm_one, norm_two, cotangent):
    seq_count, local_len, model_width = hidden_in.shape
    seq_len = segments.shape[1]
    row_count = seq_count * local_len
    groups = HEADS // KV_HEADS
    qwidth = HEADS * HEAD_DIM
    kwidth = KV_HEADS * HEAD_DIM
    score_scale = HEAD_DIM ** (-0.5)
    low = jnp.bfloat16
    wide = jnp.float32
    dp_count = lax.axis_size("dp")
    ctx_count = lax.axis_size("ctx")
    attn_shapes = ((D, qwidth), (D, kwidth), (D, kwidth), (qwidth, D))
    mlp_shapes = ((D, FFN), (D, FFN), (FFN, D))
    start_row = lax.axis_index("ctx") * local_len
    attn_whole, mlp_whole = (
        lax.all_gather(attn_flat, ("dp", "ctx"), axis=0, tiled=True),
        lax.all_gather(mlp_flat, ("dp", "ctx"), axis=0, tiled=True),
    )
    w_query, w_key, w_value, w_out = unpack_blocks(attn_whole, attn_shapes, dp_count, ctx_count)
    w_gate, w_up, w_down = unpack_blocks(mlp_whole, mlp_shapes, dp_count, ctx_count)
    pos_all = positions_of(segments)
    pos_local = lax.dynamic_slice_in_dim(pos_all, start_row, local_len, 1)
    seg_local = lax.dynamic_slice_in_dim(segments, start_row, local_len, 1)
    cosine_table, sine_table = rope_tables(pos_local.reshape(-1))
    key_index = jnp.arange(seq_len, dtype=jnp.int32)
    query_index = start_row + jnp.arange(local_len, dtype=jnp.int32)
    allowed = (seg_local[:, :, None] == segments[:, None, :]) & (
        key_index[None, None, :] <= query_index[None, :, None]
    )
    allowed = allowed[:, None, None]
    residual = hidden_in.reshape(row_count, model_width)
    inv_one, normed_one = norm_forward(residual, norm_one)
    normed_one = normed_one.astype(low)
    query = jnp.dot(normed_one, w_query, preferred_element_type=wide).reshape(
        row_count, HEADS, HEAD_DIM
    )
    key_raw = jnp.dot(normed_one, w_key, preferred_element_type=wide).reshape(
        row_count, KV_HEADS, HEAD_DIM
    )
    value_low = jnp.dot(normed_one, w_value, preferred_element_type=wide).astype(low)
    query_rot = (
        rotate(query, cosine_table, sine_table)
        .astype(low)
        .reshape(seq_count, local_len, KV_HEADS, groups, HEAD_DIM)
    )
    key_rot = rotate(key_raw, cosine_table, sine_table).astype(low)
    kv_local = jnp.concatenate(
        [
            key_rot.reshape(seq_count, local_len, kwidth),
            value_low.reshape(seq_count, local_len, kwidth),
        ],
        axis=2,
    )
    kv_whole = lax.all_gather(kv_local, "ctx", axis=1, tiled=True)
    key_whole = kv_whole[:, :, :kwidth].reshape(seq_count, seq_len, KV_HEADS, HEAD_DIM)
    value_whole = kv_whole[:, :, kwidth:].reshape(seq_count, seq_len, KV_HEADS, HEAD_DIM)
    scores = masked_scores(query_rot, key_whole, allowed, score_scale)
    row_top = jnp.max(scores, axis=-1, keepdims=True)
    log_total = row_top + jnp.log(jnp.sum(jnp.exp(scores - row_top), axis=-1, keepdims=True))
    probs_low = jnp.exp(scores - log_total).astype(low)
    head_mix = jnp.einsum("skgql,slkd->sqkgd", probs_low, value_whole, preferred_element_type=wide)
    head_mix = head_mix.reshape(row_count, qwidth).astype(low)
    middle = residual + jnp.dot(head_mix, w_out, preferred_element_type=wide)
    inv_two, normed_two = norm_forward(middle, norm_two)
    normed_two = normed_two.astype(low)
    gate_pre = jnp.dot(normed_two, w_gate, preferred_element_type=wide)
    up_proj = jnp.dot(normed_two, w_up, preferred_element_type=wide)
    gate_sigmoid = jax.nn.sigmoid(gate_pre)
    active = (gate_pre * gate_sigmoid * up_proj).astype(low)
    block_rows = middle + jnp.dot(active, w_down, preferred_element_type=wide)
    one_cols, mix_cols, two_cols, active_cols = (
        lax.all_to_all(normed_one, "ctx", split_axis=1, concat_axis=0, tiled=True),
        lax.all_to_all(head_mix, "ctx", split_axis=1, concat_axis=0, tiled=True),
        lax.all_to_all(normed_two, "ctx", split_axis=1, concat_axis=0, tiled=True),
        lax.all_to_all(active, "ctx", split_axis=1, concat_axis=0, tiled=True),
    )
    cot_rows = cotangent.reshape(row_count, model_width)
    cot_low = cot_rows.astype(low)
    grad_active = jnp.dot(cot_low, w_down.T, preferred_element_type=wide)
    grad_gate = (
        grad_active * up_proj * gate_sigmoid * (1.0 + gate_pre * (1.0 - gate_sigmoid))
    ).astype(low)
    grad_up = (grad_active * gate_pre * gate_sigmoid).astype(low)
    grad_normed_two = jnp.dot(grad_gate, w_gate.T, preferred_element_type=wide) + jnp.dot(
        grad_up, w_up.T, preferred_element_type=wide
    )
    grad_middle, grad_gain_two = norm_backward(middle, inv_two, norm_two, grad_normed_two)
    grad_middle = cot_rows + grad_middle
    grad_mid_low = grad_middle.astype(low)
    grad_mix = jnp.dot(grad_mid_low, w_out.T, preferred_element_type=wide).astype(low)
    grad_mix = grad_mix.reshape(seq_count, local_len, KV_HEADS, groups, HEAD_DIM)
    attn_probs = jnp.exp(masked_scores(query_rot, key_whole, allowed, score_scale) - log_total)
    probs_low = attn_probs.astype(low)
    grad_probs = jnp.einsum("sqkgd,slkd->skgql", grad_mix, value_whole, preferred_element_type=wide)
    grad_value_all = jnp.einsum(
        "skgql,sqkgd->slkd", probs_low, grad_mix, preferred_element_type=wide
    )
    grad_scores = attn_probs * (
        grad_probs - jnp.sum(attn_probs * grad_probs, axis=-1, keepdims=True)
    )
    grad_scores_low = (grad_scores * score_scale).astype(low)
    grad_query = jnp.einsum(
        "skgql,slkd->sqkgd", grad_scores_low, key_whole, preferred_element_type=wide
    )
    grad_key_all = jnp.einsum(
        "skgql,sqkgd->slkd", grad_scores_low, query_rot, preferred_element_type=wide
    )
    kv_terms = jnp.concatenate(
        [
            grad_key_all.reshape(seq_count, seq_len, kwidth),
            grad_value_all.reshape(seq_count, seq_len, kwidth),
        ],
        axis=2,
    )
    kv_owned = lax.psum_scatter(
        kv_terms.astype(jnp.bfloat16), "ctx", scatter_dimension=1, tiled=True
    ).astype(jnp.float32)
    grad_key = kv_owned[:, :, :kwidth].reshape(row_count, KV_HEADS, HEAD_DIM)
    grad_value = kv_owned[:, :, kwidth:].reshape(row_count, kwidth).astype(low)
    grad_query = (
        unrotate(grad_query.reshape(row_count, HEADS, HEAD_DIM), cosine_table, sine_table)
        .reshape(row_count, qwidth)
        .astype(low)
    )
    grad_key = unrotate(grad_key, cosine_table, sine_table).reshape(row_count, kwidth).astype(low)
    grad_normed_one = (
        jnp.dot(grad_query, w_query.T, preferred_element_type=wide)
        + jnp.dot(grad_key, w_key.T, preferred_element_type=wide)
        + jnp.dot(grad_value, w_value.T, preferred_element_type=wide)
    )
    grad_resid, grad_gain_one = norm_backward(residual, inv_one, norm_one, grad_normed_one)
    grad_resid = grad_middle + grad_resid
    gathered = (
        lax.all_gather(grad_query, "ctx", axis=0, tiled=True),
        lax.all_gather(grad_key, "ctx", axis=0, tiled=True),
        lax.all_gather(grad_value, "ctx", axis=0, tiled=True),
        lax.all_gather(grad_mid_low, "ctx", axis=0, tiled=True),
        lax.all_gather(grad_gate, "ctx", axis=0, tiled=True),
        lax.all_gather(grad_up, "ctx", axis=0, tiled=True),
        lax.all_gather(cot_low, "ctx", axis=0, tiled=True),
    )
    all_query, all_key, all_value, all_mid, all_gate, all_up, all_cot = gathered
    attn_terms = jnp.concatenate(
        [
            left_dot(one_cols, all_query).reshape(-1),
            left_dot(one_cols, all_key).reshape(-1),
            left_dot(one_cols, all_value).reshape(-1),
            left_dot(mix_cols, all_mid).reshape(-1),
        ]
    ).reshape(-1, 128)
    mlp_terms = jnp.concatenate(
        [
            left_dot(two_cols, all_gate).reshape(-1),
            left_dot(two_cols, all_up).reshape(-1),
            left_dot(active_cols, all_cot).reshape(-1),
        ]
    ).reshape(-1, 128)
    attn_grad, mlp_grad = (
        lax.psum_scatter(
            attn_terms.astype(jnp.bfloat16), "dp", scatter_dimension=0, tiled=True
        ).astype(jnp.float32),
        lax.psum_scatter(
            mlp_terms.astype(jnp.bfloat16), "dp", scatter_dimension=0, tiled=True
        ).astype(jnp.float32),
    )
    gain_sums = lax.psum(jnp.stack([grad_gain_one, grad_gain_two]), ("dp", "ctx"))
    return (
        block_rows.reshape(seq_count, local_len, model_width),
        grad_resid.reshape(seq_count, local_len, model_width),
        attn_grad,
        mlp_grad,
        gain_sums[0],
        gain_sums[1],
    )


def solution(mesh):
    in_specs = (
        P("dp", "ctx", None),
        P("dp", None),
        P(("dp", "ctx"), None),
        P(("dp", "ctx"), None),
        P(),
        P(),
        P("dp", "ctx", None),
    )
    out_specs = (
        P("dp", "ctx", None),
        P("dp", "ctx", None),
        P(("dp", "ctx"), None),
        P(("dp", "ctx"), None),
        P(),
        P(),
    )
    return jax.shard_map(body, mesh=mesh, in_specs=in_specs, out_specs=out_specs, check_vma=False)
```

profile of v0, /device:TPU:0, one launch (start us, length us, event | category | flops | bytes accessed | tf_op | source)
XLA Modules:
  0.0 637.0 jit_solution(12020990512070765392)
XLA Ops:
  14.3 63.6 %all-gather.6.cloned.1.call-done = bf16[19200,128]{1,0:T(8,128)(2,1)} async-done(((bf16[600,128]{1,0:T(8,128)(2,1)}), bf16[19200,128]{1,0:T(8,128)(2,1)}) %all-gather.6.cloned.1.call-update) | async-done | bytes 4915216 | tf_op jit(solution)/shard_map/all_gather | solution.py:110
  77.9 7.6 %reshape.572 = bf16[8,4,76800]{2,1,0:T(4,128)(2,1)} reshape(bf16[19200,128]{1,0:T(8,128)(2,1)} %all-gather.6.cloned.1.call-done) | data formatting | bytes 9830400 | tf_op jit(solution)/shard_map/reshape | solution.py:55
  85.5 3.7 fusion.52
  89.2 3.4 reshape.612
  92.6 2.7 fusion.53
  97.1 4.5 reshape.581
  102.8 2.6 reshape.575
  107.3 3.4 reshape.579
  110.7 2.5 copy.58
  116.1 26.2 %all_gather.31 = bf16[1,512,640]{1,2,0:T(8,128)(2,1)S(1)} all-gather(bf16[1,128,640]{1,2,0:T(8,128)(2,1)S(1)} %pad_maximum_fusion.3), channel_id=1, replica_groups=mesh['dp'=8,'ctx'=4] {'ctx'}, dimensions={1}, use_global_device_ids=true | all-gather | bytes 819200 | tf_op jit(solution)/shard_map/all_gather | solution.py:148
  151.4 41.2 %all-gather.8.cloned.1.call-done = bf16[57600,128]{1,0:T(8,128)(2,1)} async-done(((bf16[1800,128]{1,0:T(8,128)(2,1)}), bf16[57600,128]{1,0:T(8,128)(2,1)}) %all-gather.8.cloned.1.call-update) | async-done | bytes 14745616 | tf_op jit(solution)/shard_map/all_gather | solution.py:111
  192.7 14.8 %reshape.582 = bf16[8,4,230400]{2,1,0:T(4,128)(2,1)} reshape(bf16[57600,128]{1,0:T(8,128)(2,1)} %all-gather.8.cloned.1.call-done) | data formatting | bytes 29491200 | tf_op jit(solution)/shard_map/reshape | solution.py:55
  207.4 13.3 %fusion.51 = (bf16[4,614400]{1,0:T(4,128)(2,1)}, bf16[4,614400]{1,0:T(4,128)(2,1)}, bf16[4,614400]{1,0:T(4,128)(2,1)}) fusion(bf16[4,1843200]{1,0:T(4,128)(2,1)} %bitcast.241), kind=kLoop, calls=%fused_computation.122 | loop fusion | bytes 29491200 | tf_op jit(solution)/shard_map/slice | solution.py:60
  220.7 9.6 %reshape.614 = bf16[2457600]{0:T(1024)(128)(2,1)} reshape(bf16[4,614400]{1,0:T(4,128)(2,1)} %get-tuple-element.12) | data formatting | bytes 9830400
  230.2 9.7 %reshape.586 = bf16[2560,960]{1,0:T(8,128)(2,1)} reshape(bf16[2457600]{0:T(1024)(128)(2,1)} %reshape.614) | data formatting | bytes 9830400 | tf_op jit(solution)/shard_map/reshape | solution.py:60
  239.9 9.2 %reshape.585 = bf16[960,2560]{1,0:T(8,128)(2,1)} reshape(bf16[4,614400]{1,0:T(4,128)(2,1)} %get-tuple-element.13) | data formatting | bytes 9830400 | tf_op jit(solution)/shard_map/reshape | solution.py:60
  249.1 9.2 %reshape.584 = bf16[960,2560]{1,0:T(8,128)(2,1)} reshape(bf16[4,614400]{1,0:T(4,128)(2,1)} %get-tuple-element.14) | data formatting | bytes 9830400 | tf_op jit(solution)/shard_map/reshape | solution.py:60
  258.3 3.5 fusion.59
  264.5 3.9 multiply_convert_fusion
  268.4 4.1 fusion.60
  272.6 4.3 multiply_reduce_fusion
  285.1 3.7 copy.78
  288.9 2.3 copy.112
  293.8 31.8 %all_gather.39 = bf16[512,960]{0,1:T(8,128)(2,1)} all-gather(bf16[128,960]{0,1:T(8,128)(2,1)S(1)} %bitcast_convert_fusion), channel_id=1, replica_groups=mesh['dp'=8,'ctx'=4] {'ctx'}, dimensions={0}, use_global_device_ids=true | all-gather | bytes 1228800 | tf_op jit(solution)/shard_map/all_gather | solution.py:234
  325.6 3.4 all-to-all-start.1
  329.6 49.0 %all_gather.36 = bf16[512,960]{0,1:T(8,128)(2,1)} all-gather(bf16[128,960]{0,1:T(8,128)(2,1)S(1)} %copy-done.20), channel_id=1, replica_groups=mesh['dp'=8,'ctx'=4] {'ctx'}, dimensions={0}, use_global_device_ids=true | all-gather | bytes 1228800 | tf_op jit(solution)/shard_map/all_gather | solution.py:231
  378.6 15.8 %all-to-all-start = ((bf16[128,4,240]{0,2,1:T(8,128)(2,1)}), bf16[128,4,240]{0,2,1:T(8,128)(2,1)S(1)}, u32[]{:S(2)}, u32[]{:S(2)}) async-start(bf16[128,4,240]{0,2,1:T(8,128)(2,1)} %multiply_convert_fusion.3), calls=%async_computation | async-start | bytes 491520 | tf_op jit(solution)/shard_map/all_to_all | solution.py:166
  394.5 2.4 convolution_convert_fusion.3
  398.9 2.4 reshape.598
  401.3 2.9 fusion.61
  404.2 5.1 all-to-all-start.3
  410.5 58.9 %all_gather.33 = bf16[512,960]{0,1:T(8,128)(2,1)S(1)} all-gather(bf16[128,960]{0,1:T(8,128)(2,1)S(1)} %bitcast.259), channel_id=1, replica_groups=mesh['dp'=8,'ctx'=4] {'ctx'}, dimensions={0}, use_global_device_ids=true | all-gather | bytes 1228800 | tf_op jit(solution)/shard_map/all_gather | solution.py:228
  470.6 2.4 reshape.595
  473.0 12.6 %all-to-all-start.2 = ((bf16[128,4,240]{0,2,1:T(8,128)(2,1)}), bf16[128,4,240]{0,2,1:T(8,128)(2,1)S(1)}, u32[]{:S(2)}, u32[]{:S(2)}) async-start(bf16[128,4,240]{0,2,1:T(8,128)(2,1)} %bitcast.72), calls=%async_computation.2 | async-start | bytes 491520 | tf_op jit(solution)/shard_map/all_to_all | solution.py:168
  485.6 3.4 convolution_convert_fusion.2
  489.0 2.5 copy.69
  491.5 3.8 concatenate.68
  502.0 14.0 %all_gather.34 = bf16[512,320]{0,1:T(8,128)(2,1)S(1)} all-gather(bf16[128,320]{0,1:T(8,128)(2,1)S(1)} %bitcast.270), channel_id=1, replica_groups=mesh['dp'=8,'ctx'=4] {'ctx'}, dimensions={0}, use_global_device_ids=true | all-gather | bytes 409600 | tf_op jit(solution)/shard_map/all_gather | solution.py:229
  520.4 13.2 %all-gather = bf16[1,512,320]{1,2,0:T(8,128)(2,1)S(1)} all-gather(bf16[1,128,320]{1,2,0:T(8,128)(2,1)} %slice.122), channel_id=2, replica_groups=mesh['dp'=8,'ctx'=4] {'ctx'}, dimensions={1}, use_global_device_ids=true | all-gather | bytes 409600 | tf_op jit(solution)/shard_map/all_gather | solution.py:230
  536.6 2.4 maximum_bitcast_fusion
  539.1 3.6 convolution_convert_fusion
  542.7 3.7 convolution_convert_fusion.1
  546.4 3.8 concatenate.67
  550.2 3.7 concatenate.66
  553.9 6.0 pad_maximum_fusion
  559.9 5.3 fusion.9
  566.9 39.3 %psum.7 = f32[2,960]{1,0:T(2,128)S(1)} all-reduce(f32[2,960]{1,0:T(2,128)S(1)} %pad_maximum_fusion.7), channel_id=1, replica_groups=mesh['dp'=8,'ctx'=4] {'dp','ctx'}, use_global_device_ids=true, to_apply=%region_13.14 | all-reduce | flops 1920 | bytes 15360 | tf_op jit(solution)/shard_map/psum | solution.py:260
  609.5 18.5 %reduce-scatter.14.cloned.1.call-done = bf16[1800,128]{1,0:T(8,128)(2,1)} async-done(((bf16[14400,128]{1,0:T(8,128)(2,1)}), bf16[1800,128]{1,0:T(8,128)(2,1)}) %reduce-scatter.14.cloned.1.call-update) | async-done | bytes 460816
  (170 shorter events, 63.2 us)
Async XLA Ops:
  7.2 70.7 %all-gather.6.cloned.1.call-start = ((), (), s32[]{:S(2)}) async-start(), calls=%async_computation.7 | async-start | bytes 5068800 | tf_op jit(solution)/shard_map/all_gather | solution.py:110
  7.9 184.8 %all-gather.8.cloned.1.call-start = ((), (), s32[]{:S(2)}) async-start(), calls=%async_computation.8 | async-start | bytes 15206400 | tf_op jit(solution)/shard_map/all_gather | solution.py:111
  8.6 486.6 %reduce-scatter.10.cloned.1.call-start = ((), (), s32[]{:S(2)}) async-start(), calls=%async_computation.11 | async-start | bytes 819200
  10.4 75.1 %copy-start.33 = (f32[128]{0:T(128)}, f32[128]{0:T(128)S(1)}, u32[]{:S(2)}) copy-start(f32[128]{0:T(128)S(1)} %get-tuple-element.37) | copy-start | bytes 1540
  97.1 8.3 %copy-start.10 = (bf16[960,320]{1,0:T(8,128)(2,1)}, bf16[960,320]{1,0:T(8,128)(2,1)S(1)}, u32[]{:S(2)}) copy-start(bf16[960,320]{1,0:T(8,128)(2,1)S(1)} %reshape.574) | copy-start | bytes 1843204
  110.7 4.1 copy-start.12
  113.2 2.1 copy-start.9
  116.1 27.8 %copy-start.25 = (bf16[128,15,32]{0,2,1:T(8,128)(2,1)}, bf16[128,15,32]{0,2,1:T(8,128)(2,1)S(1)}, u32[]{:S(2)}) copy-start(bf16[128,15,32]{0,2,1:T(8,128)(2,1)S(1)} %get-tuple-element.26) | copy-start | bytes 368644
  116.1 27.8 %copy-start.27 = (bf16[128,15,32]{0,2,1:T(8,128)(2,1)}, bf16[128,15,32]{0,2,1:T(8,128)(2,1)S(1)}, u32[]{:S(2)}) copy-start(bf16[128,15,32]{0,2,1:T(8,128)(2,1)S(1)} %get-tuple-element.27) | copy-start | bytes 368644
  142.4 2.1 copy-start.15
  143.9 2.5 copy-start
  144.5 2.9 copy-start.3
  144.5 3.1 copy-start.6
  146.4 4.2 copy-start.32
  149.5 0.8 copy-start.7
  249.1 15.3 %slice-start = ((s8[5242880]{0:T(1024)(128)(4,1)}), s8[1048576]{0:T(1024)(128)(4,1)S(1)}, s32[]{:S(2)}) async-start(s8[5242880]{0:T(1024)(128)(4,1)} %bitcast.242), calls=%async_computation.14 | async-start | bytes 2097152
  258.3 4.0 copy-start.2
  258.3 6.1 slice-start.1
  262.3 2.2 copy-start.21
  268.4 4.1 copy-start.8
  268.4 4.1 copy-start.36
  272.5 4.4 copy-start.22
  272.6 4.4 copy-start.37
  272.6 6.1 copy-start.4
  276.9 2.4 copy-start.1
  279.3 1.0 copy-start.16
  281.2 2.3 copy-start.26
  281.2 2.3 copy-start.28
  282.2 1.3 copy-start.5
  285.1 6.6 %copy-start.31 = (f32[960]{0:T(1024)S(1)}, f32[960]{0:T(1024)}, u32[]{:S(2)}) copy-start(f32[960]{0:T(1024)} %param.11) | copy-start | bytes 11524
  285.1 7.8 %copy-start.34 = (f32[128]{0:T(128)S(1)}, f32[128]{0:T(128)}, u32[]{:S(2)}) copy-start(f32[128]{0:T(128)} %copy-done.33) | copy-start | bytes 1540
  291.1 38.5 %copy-start.20 = (bf16[128,960]{0,1:T(8,128)(2,1)S(1)}, bf16[128,960]{0,1:T(8,128)(2,1)}, u32[]{:S(2)}) copy-start(bf16[128,960]{0,1:T(8,128)(2,1)} %copy-done.19) | copy-start | bytes 737284
  291.2 247.9 %all-gather.12.cloned.1.call-start = ((), (), s32[]{:S(2)}) async-start(), calls=%async_computation.10 | async-start | bytes 3276800 | tf_op jit(solution)/shard_map/all_gather | solution.py:233
  325.6 53.0 %all-to-all-start.1 = ((bf16[128,4,240]{0,2,1:T(8,128)(2,1)}), bf16[128,4,240]{0,2,1:T(8,128)(2,1)S(1)}, u32[]{:S(2)}, u32[]{:S(2)}) async-start(bf16[128,4,240]{0,2,1:T(8,128)(2,1)} %bitcast.69), calls=%async_computation.1 | async-start | bytes 491520 | tf_op jit(solution)/shard_map/all_to_all | solution.py:167
  329.0 213.7 %all-gather.10.cloned.1.call-start = ((), (), s32[]{:S(2)}) async-start(), calls=%async_computation.9 | async-start | bytes 3276800 | tf_op jit(solution)/shard_map/all_gather | solution.py:232
  378.6 25.6 %all-to-all-start = ((bf16[128,4,240]{0,2,1:T(8,128)(2,1)}), bf16[128,4,240]{0,2,1:T(8,128)(2,1)S(1)}, u32[]{:S(2)}, u32[]{:S(2)}) async-start(bf16[128,4,240]{0,2,1:T(8,128)(2,1)} %multiply_convert_fusion.3), calls=%async_computation | async-start | bytes 491520 | tf_op jit(solution)/shard_map/all_to_all | solution.py:166
  404.2 68.8 %all-to-all-start.3 = ((bf16[128,4,640]{2,0,1:T(8,128)(2,1)}), bf16[128,4,640]{2,0,1:T(8,128)(2,1)}, u32[]{:S(2)}, u32[]{:S(2)}) async-start(bf16[128,4,640]{2,0,1:T(8,128)(2,1)} %bitcast.255), calls=%async_computation.3 | async-start | bytes 1310720 | tf_op jit(solution)/shard_map/all_to_all | solution.py:169
  410.4 62.5 %copy-start.17 = (bf16[128,15,64]{0,2,1:T(8,128)(2,1)}, bf16[128,15,64]{0,2,1:T(8,128)(2,1)S(1)}, u32[]{:S(2)}) copy-start(bf16[128,15,64]{0,2,1:T(8,128)(2,1)S(1)} %maximum_convert_fusion) | copy-start | bytes 737284
  473.0 66.1 %all-to-all-start.2 = ((bf16[128,4,240]{0,2,1:T(8,128)(2,1)}), bf16[128,4,240]{0,2,1:T(8,128)(2,1)S(1)}, u32[]{:S(2)}, u32[]{:S(2)}) async-start(bf16[128,4,240]{0,2,1:T(8,128)(2,1)} %bitcast.72), calls=%async_computation.2 | async-start | bytes 491520 | tf_op jit(solution)/shard_map/all_to_all | solution.py:168
  485.6 122.2 %reduce-scatter.12.cloned.1.call-start = ((), (), s32[]{:S(2)}) async-start(), calls=%async_computation.12 | async-start | bytes 1382400
  539.0 88.9 %reduce-scatter.14.cloned.1.call-start = ((), (), s32[]{:S(2)}) async-start(), calls=%async_computation.13 | async-start | bytes 4147200
  559.9 5.3 copy-start.13
  559.9 5.3 copy-start.24
  559.9 5.7 copy-start.11
  559.9 5.7 copy-start.30
  565.2 0.9 copy-start.18
  565.6 41.2 %copy-start.23 = (f32[128,960]{0,1:T(8,128)S(1)}, f32[128,960]{0,1:T(8,128)}, u32[]{:S(2)}) copy-start(f32[128,960]{0,1:T(8,128)} %get-tuple-element.11) | copy-start | bytes 1474564
  565.6 41.2 %copy-start.38 = (f32[128]{0:T(128)S(1)}, f32[128]{0:T(128)}, u32[]{:S(2)}) copy-start(f32[128]{0:T(128)} %get-tuple-element.36) | copy-start | bytes 1540
  (4 other events, 2.6 us)
Sparse Core Ops, SparseCore 0:
  10.8 66.9 all-gather.5
  80.7 111.8 all-gather.7
  291.3 28.9 reduce-scatter.9
  321.7 74.3 all-gather.11
  397.5 83.4 all-gather.9
  539.1 35.7 reduce-scatter.11
  578.4 49.5 reduce-scatter.13
where the time goes:
time: 646 us; the launch traced here: 637 us
  blocking collectives  232 us (36%)
  local copies, waits for them, and re-layouts  147 us (23%)
  waiting for transfers between devices  126 us (20%)
  matrix products  53.7 us (8%)
  starting transfers between devices  37.2 us (6%)
  other arithmetic  26 us (4%)
  between operations  15 us (2%)
    all_gather x1, waiting for transfers between devices, body(): lax.all_gather(attn_flat, ('dp', 'ctx'), axis=0, tiled=True)  63.6 us
    all_gather x1, blocking collectives, body(): lax.all_gather(grad_query, 'ctx', axis=0, tiled=True)  58.9 us
    all_gather x1, blocking collectives, body(): lax.all_gather(grad_mid_low, 'ctx', axis=0, tiled=True)  49 us
    all_gather x1, waiting for transfers between devices, body(): lax.all_gather(mlp_flat, ('dp', 'ctx'), axis=0, tiled=True)  41.2 us
    reshape x7, local copies, waits for them, and re-layouts, unpack_blocks(): pieces[:, offset:offset + length].reshape(height, width_cols)  40.4 us
    psum x1, blocking collectives, body(): lax.psum(jnp.stack([grad_gain_one, grad_gain_two]), ('dp', 'ctx'))  39.3 us
    all_gather x1, blocking collectives, body(): lax.all_gather(cot_low, 'ctx', axis=0, tiled=True)  31.8 us
    unnamed x89, local copies, waits for them, and re-layouts  31 us
  transfers between devices with their start and end apart: 11, of which 3 were waited for; matrix products, arithmetic and copies ran while one was open for 19% of the time, Pallas kernels for 0%

commit v1 on v0

--- a/solution.py
+++ b/solution.py
@@ -2,6 +2,7 @@
 import jax.numpy as jnp
 from jax import lax
 from jax.sharding import PartitionSpec as P
+from jax.lax import axis_index, axis_size, ppermute
 
 D = 960
 HEADS = 15
@@ -224,8 +225,29 @@
     )
     grad_resid, grad_gain_one = norm_backward(residual, inv_one, norm_one, grad_normed_one)
     grad_resid = grad_middle + grad_resid
+
+    def axis_part_mark(a0, bus_axis):
+        d_next, reply, before = (axis_size(bus_axis), axis_index(bus_axis), a0.shape[0])
+        buffers = [(ii, (ii + 1) % d_next) for ii in range(d_next)]
+        stack_in = [(ii, (ii - 1) % d_next) for ii in range(d_next)]
+        current_arr = jnp.zeros((*a0.shape[:0], d_next * before, *a0.shape[1:]), a0.dtype)
+        current_arr = lax.dynamic_update_slice_in_dim(current_arr, a0, reply * before, axis=0)
+        out_arr = block_next = a0
+        e_now = d_next // 2
+        for m in [*range(1, e_now + 1)]:
+            out_arr = ppermute(out_arr, bus_axis, buffers)
+            current_arr = lax.dynamic_update_slice_in_dim(
+                current_arr, out_arr, (reply - m) % d_next * before, axis=0
+            )
+            if m < d_next - e_now:
+                block_next = ppermute(block_next, bus_axis, stack_in)
+                current_arr = lax.dynamic_update_slice_in_dim(
+                    current_arr, block_next, (reply + m) % d_next * before, axis=0
+                )
+        return current_arr
+
     gathered = (
-        lax.all_gather(grad_query, "ctx", axis=0, tiled=True),
+        axis_part_mark(grad_query, "ctx"),
         lax.all_gather(grad_key, "ctx", axis=0, tiled=True),
         lax.all_gather(grad_value, "ctx", axis=0, tiled=True),
         lax.all_gather(grad_mid_low, "ctx", axis=0, tiled=True),

time: 646 us -> 626 us (0.969)
  blocking collectives: 232 us -> 184 us
  waiting for transfers between devices: 126 us -> 140 us
  starting transfers between devices: 37.2 us -> 45.1 us
    all_gather x1 -> x0, blocking collectives: 58.9 us -> none  [body(): lax.all_gather(grad_query, 'ctx', axis=0, tiled=True)]
    ppermute x0 -> x3, waiting for transfers between devices: none -> 15.7 us  [the longest x2 15.7 us: axis_part_mark(): out_arr = ppermute(out_arr, bus_axis, buffers)]
    all_to_all x1, starting transfers between devices: 15.8 us -> 3.41 us  [body(): lax.all_to_all(normed_one, 'ctx', split_axis=1, concat_axis=0, tiled=True)]
    all_gather x1, blocking collectives: 49 us -> 60.4 us  [body(): lax.all_gather(grad_mid_low, 'ctx', axis=0, tiled=True)]
    all_to_all x1, starting transfers between devices: 12.6 us -> 21.6 us  [body(): lax.all_to_all(normed_two, 'ctx', split_axis=1, concat_axis=0, tiled=True)]
  transfers between devices with their start and end apart: 11 -> 14, of which waited for: 3 -> 4; matrix products, arithmetic and copies ran while one was open for 19% -> 21% of each run, Pallas kernels for 0% -> 0%
where the time goes in v1:
time: 626 us; the launch traced here: 617 us
  blocking collectives  184 us (29%)
  local copies, waits for them, and re-layouts  153 us (24%)
  waiting for transfers between devices  140 us (22%)
  matrix products  53.7 us (9%)
  starting transfers between devices  45.1 us (7%)
  other arithmetic  25.6 us (4%)
  between operations  15 us (2%)
    all_gather x1, waiting for transfers between devices, body(): lax.all_gather(attn_flat, ('dp', 'ctx'), axis=0, tiled=True)  63.6 us
    all_gather x1, blocking collectives, body(): lax.all_gather(grad_mid_low, 'ctx', axis=0, tiled=True)  60.4 us
    all_gather x1, waiting for transfers between devices, body(): lax.all_gather(mlp_flat, ('dp', 'ctx'), axis=0, tiled=True)  42.1 us
    reshape x7, local copies, waits for them, and re-layouts, unpack_blocks(): pieces[:, offset:offset + length].reshape(height, width_cols)  40.5 us
    psum x1, blocking collectives, body(): lax.psum(jnp.stack([grad_gain_one, grad_gain_two]), ('dp', 'ctx'))  38.6 us
    all_gather x1, blocking collectives, body(): lax.all_gather(cot_low, 'ctx', axis=0, tiled=True)  32.5 us
    unnamed x89, local copies, waits for them, and re-layouts  31.5 us
    all_gather x1, blocking collectives, body(): kv_whole = lax.all_gather(kv_local, 'ctx', axis=1, tiled=True)  26 us
  transfers between devices with their start and end apart: 14, of which 4 were waited for; matrix products, arithmetic and copies ran while one was open for 21% of the time, Pallas kernels for 0%

profile of v1, /device:TPU:0, one launch (start us, length us, event | category | flops | bytes accessed | tf_op | source)
XLA Modules:
  0.0 617.3 jit_solution(13771331285308366346)
XLA Ops:
  14.3 63.6 %all-gather.6.cloned.1.call-done = bf16[19200,128]{1,0:T(8,128)(2,1)} async-done(((bf16[600,128]{1,0:T(8,128)(2,1)}), bf16[19200,128]{1,0:T(8,128)(2,1)}) %all-gather.6.cloned.1.call-update) | async-done | bytes 4915216 | tf_op jit(solution)/shard_map/all_gather | solution.py:111
  77.9 7.6 %reshape.572 = bf16[8,4,76800]{2,1,0:T(4,128)(2,1)} reshape(bf16[19200,128]{1,0:T(8,128)(2,1)} %all-gather.6.cloned.1.call-done) | data formatting | bytes 9830400 | tf_op jit(solution)/shard_map/reshape | solution.py:56
  85.5 3.7 fusion.54
  89.2 3.4 reshape.612
  92.6 2.7 fusion.55
  97.1 4.6 reshape.581
  102.8 2.6 reshape.575
  107.3 3.5 reshape.579
  110.8 2.5 copy.58
  116.1 26.0 %all_gather.28 = bf16[1,512,640]{1,2,0:T(8,128)(2,1)S(1)} all-gather(bf16[1,128,640]{1,2,0:T(8,128)(2,1)S(1)} %pad_maximum_fusion.3), channel_id=1, replica_groups=mesh['dp'=8,'ctx'=4] {'ctx'}, dimensions={1}, use_global_device_ids=true | all-gather | bytes 819200 | tf_op jit(solution)/shard_map/all_gather | solution.py:149
  150.4 42.1 %all-gather.8.cloned.1.call-done = bf16[57600,128]{1,0:T(8,128)(2,1)} async-done(((bf16[1800,128]{1,0:T(8,128)(2,1)}), bf16[57600,128]{1,0:T(8,128)(2,1)}) %all-gather.8.cloned.1.call-update) | async-done | bytes 14745616 | tf_op jit(solution)/shard_map/all_gather | solution.py:112
  192.5 14.8 %reshape.582 = bf16[8,4,230400]{2,1,0:T(4,128)(2,1)} reshape(bf16[57600,128]{1,0:T(8,128)(2,1)} %all-gather.8.cloned.1.call-done) | data formatting | bytes 29491200 | tf_op jit(solution)/shard_map/reshape | solution.py:56
  207.3 13.3 %fusion.53 = (bf16[4,614400]{1,0:T(4,128)(2,1)}, bf16[4,614400]{1,0:T(4,128)(2,1)}, bf16[4,614400]{1,0:T(4,128)(2,1)}) fusion(bf16[4,1843200]{1,0:T(4,128)(2,1)} %bitcast.241), kind=kLoop, calls=%fused_computation.128 | loop fusion | bytes 29491200 | tf_op jit(solution)/shard_map/slice | solution.py:61
  220.5 9.6 %reshape.614 = bf16[2457600]{0:T(1024)(128)(2,1)} reshape(bf16[4,614400]{1,0:T(4,128)(2,1)} %get-tuple-element.12) | data formatting | bytes 9830400
  230.1 9.7 %reshape.586 = bf16[2560,960]{1,0:T(8,128)(2,1)} reshape(bf16[2457600]{0:T(1024)(128)(2,1)} %reshape.614) | data formatting | bytes 9830400 | tf_op jit(solution)/shard_map/reshape | solution.py:61
  239.8 9.2 %reshape.585 = bf16[960,2560]{1,0:T(8,128)(2,1)} reshape(bf16[4,614400]{1,0:T(4,128)(2,1)} %get-tuple-element.13) | data formatting | bytes 9830400 | tf_op jit(solution)/shard_map/reshape | solution.py:61
  249.0 9.2 %reshape.584 = bf16[960,2560]{1,0:T(8,128)(2,1)} reshape(bf16[4,614400]{1,0:T(4,128)(2,1)} %get-tuple-element.14) | data formatting | bytes 9830400 | tf_op jit(solution)/shard_map/reshape | solution.py:61
  258.2 3.5 fusion.61
  264.4 3.9 multiply_convert_fusion
  268.3 4.1 fusion.62
  272.4 4.3 multiply_reduce_fusion
  285.0 3.7 copy.78
  292.5 3.4 all-to-all-start
  297.1 32.5 %all_gather.35 = bf16[512,960]{0,1:T(8,128)(2,1)} all-gather(bf16[128,960]{0,1:T(8,128)(2,1)S(1)} %bitcast_convert_fusion), channel_id=1, replica_groups=mesh['dp'=8,'ctx'=4] {'ctx'}, dimensions={0}, use_global_device_ids=true | all-gather | bytes 1228800 | tf_op jit(solution)/shard_map/all_gather | solution.py:256
  333.0 3.4 collective-permute-start
  337.3 5.2 all-to-all-start.1
  342.6 60.4 %all_gather.32 = bf16[512,960]{0,1:T(8,128)(2,1)} all-gather(bf16[128,960]{0,1:T(8,128)(2,1)S(1)} %copy-done.19), channel_id=1, replica_groups=mesh['dp'=8,'ctx'=4] {'ctx'}, dimensions={0}, use_global_device_ids=true | all-gather | bytes 1228800 | tf_op jit(solution)/shard_map/all_gather | solution.py:253
  402.9 8.8 %all-to-all-start.3 = ((bf16[128,4,640]{2,0,1:T(8,128)(2,1)}), bf16[128,4,640]{2,0,1:T(8,128)(2,1)}, u32[]{:S(2)}, u32[]{:S(2)}) async-start(bf16[128,4,640]{2,0,1:T(8,128)(2,1)} %bitcast.255), calls=%async_computation.3 | async-start | bytes 1310720 | tf_op jit(solution)/shard_map/all_to_all | solution.py:170
  411.8 2.6 convolution_convert_fusion.3
  419.1 2.4 reshape.598
  424.9 15.7 %collective-permute-done.2 = bf16[128,960]{0,1:T(8,128)(2,1)S(1)} collective-permute-done((bf16[128,960]{0,1:T(8,128)(2,1)}, bf16[128,960]{0,1:T(8,128)(2,1)S(1)}, u32[]{:S(2)}, u32[]{:S(2)}) %collective-permute-start.2) | collective-permute-done | bytes 245792 | tf_op jit(solution)/shard_map/ppermute | solution.py:238
  441.3 2.4 convolution_convert_fusion.4
  443.8 2.4 reshape.595
  446.2 21.6 %all-to-all-start.2 = ((bf16[128,4,240]{0,2,1:T(8,128)(2,1)}), bf16[128,4,240]{0,2,1:T(8,128)(2,1)S(1)}, u32[]{:S(2)}, u32[]{:S(2)}) async-start(bf16[128,4,240]{0,2,1:T(8,128)(2,1)} %bitcast.72), calls=%async_computation.2 | async-start | bytes 491520 | tf_op jit(solution)/shard_map/all_to_all | solution.py:169
  467.8 3.4 convolution_convert_fusion.2
  471.2 2.6 copy.69
  473.8 3.8 concatenate.68
  484.3 13.6 %all_gather.30 = bf16[512,320]{0,1:T(8,128)(2,1)S(1)} all-gather(bf16[128,320]{0,1:T(8,128)(2,1)S(1)} %bitcast.270), channel_id=1, replica_groups=mesh['dp'=8,'ctx'=4] {'ctx'}, dimensions={0}, use_global_device_ids=true | all-gather | bytes 409600 | tf_op jit(solution)/shard_map/all_gather | solution.py:251
  502.4 13.2 %all-gather = bf16[1,512,320]{1,2,0:T(8,128)(2,1)S(1)} all-gather(bf16[1,128,320]{1,2,0:T(8,128)(2,1)} %slice.122), channel_id=2, replica_groups=mesh['dp'=8,'ctx'=4] {'ctx'}, dimensions={1}, use_global_device_ids=true | all-gather | bytes 409600 | tf_op jit(solution)/shard_map/all_gather | solution.py:252
  518.6 2.4 maximum_bitcast_fusion
  521.1 3.6 convolution_convert_fusion
  524.7 3.7 convolution_convert_fusion.1
  528.4 3.8 concatenate.67
  532.1 3.7 concatenate.66
  535.8 6.0 pad_maximum_fusion
  541.9 5.4 fusion.9
  549.8 38.6 %psum.7 = f32[2,960]{1,0:T(2,128)S(1)} all-reduce(f32[2,960]{1,0:T(2,128)S(1)} %pad_maximum_fusion.7), channel_id=1, replica_groups=mesh['dp'=8,'ctx'=4] {'dp','ctx'}, use_global_device_ids=true, to_apply=%region_13.14 | all-reduce | flops 1920 | bytes 15360 | tf_op jit(solution)/shard_map/psum | solution.py:282
  591.6 16.7 %reduce-scatter.14.cloned.1.call-done = bf16[1800,128]{1,0:T(8,128)(2,1)} async-done(((bf16[14400,128]{1,0:T(8,128)(2,1)}), bf16[1800,128]{1,0:T(8,128)(2,1)}) %reduce-scatter.14.cloned.1.call-update) | async-done | bytes 460816
  (180 shorter events, 73.5 us)
Async XLA Ops:
  7.2 70.7 %all-gather.6.cloned.1.call-start = ((), (), s32[]{:S(2)}) async-start(), calls=%async_computation.7 | async-start | bytes 5068800 | tf_op jit(solution)/shard_map/all_gather | solution.py:111
  7.9 184.6 %all-gather.8.cloned.1.call-start = ((), (), s32[]{:S(2)}) async-start(), calls=%async_computation.8 | async-start | bytes 15206400 | tf_op jit(solution)/shard_map/all_gather | solution.py:112
  8.6 468.9 %reduce-scatter.10.cloned.1.call-start = ((), (), s32[]{:S(2)}) async-start(), calls=%async_computation.11 | async-start | bytes 819200
  10.4 75.1 %copy-start.33 = (f32[128]{0:T(128)}, f32[128]{0:T(128)S(1)}, u32[]{:S(2)}) copy-start(f32[128]{0:T(128)S(1)} %get-tuple-element.37) | copy-start | bytes 1540
  97.1 8.3 %copy-start.10 = (bf16[960,320]{1,0:T(8,128)(2,1)}, bf16[960,320]{1,0:T(8,128)(2,1)S(1)}, u32[]{:S(2)}) copy-start(bf16[960,320]{1,0:T(8,128)(2,1)S(1)} %reshape.574) | copy-start | bytes 1843204
  110.8 4.1 copy-start.12
  113.3 2.1 copy-start.9
  116.1 27.6 %copy-start.25 = (bf16[128,15,32]{0,2,1:T(8,128)(2,1)}, bf16[128,15,32]{0,2,1:T(8,128)(2,1)S(1)}, u32[]{:S(2)}) copy-start(bf16[128,15,32]{0,2,1:T(8,128)(2,1)S(1)} %get-tuple-element.26) | copy-start | bytes 368644
  116.1 27.6 %copy-start.27 = (bf16[128,15,32]{0,2,1:T(8,128)(2,1)}, bf16[128,15,32]{0,2,1:T(8,128)(2,1)S(1)}, u32[]{:S(2)}) copy-start(bf16[128,15,32]{0,2,1:T(8,128)(2,1)S(1)} %get-tuple-element.27) | copy-start | bytes 368644
  142.2 2.1 copy-start.15
  143.8 2.5 copy-start
  144.3 2.9 copy-start.4
  144.3 3.2 copy-start.6
  146.2 2.2 copy-start.20
  146.2 3.2 copy-start.32
  249.0 15.3 %slice-start = ((s8[5242880]{0:T(1024)(128)(4,1)}), s8[1048576]{0:T(1024)(128)(4,1)S(1)}, s32[]{:S(2)}) async-start(s8[5242880]{0:T(1024)(128)(4,1)} %bitcast.242), calls=%async_computation.14 | async-start | bytes 2097152
  258.2 4.0 copy-start.2
  258.2 6.1 slice-start.1
  262.2 2.2 copy-start.21
  268.3 4.1 copy-start.8
  268.3 4.1 copy-start.36
  272.4 4.4 copy-start.22
  272.4 4.4 copy-start.37
  272.4 6.1 copy-start.5
  276.7 2.4 copy-start.1
  281.0 2.3 copy-start.26
  281.1 2.3 copy-start.28
  285.0 6.6 %copy-start.31 = (f32[960]{0:T(1024)S(1)}, f32[960]{0:T(1024)}, u32[]{:S(2)}) copy-start(f32[960]{0:T(1024)} %param.11) | copy-start | bytes 11524
  285.0 6.7 %copy-start.34 = (f32[128]{0:T(128)S(1)}, f32[128]{0:T(128)}, u32[]{:S(2)}) copy-start(f32[128]{0:T(128)} %copy-done.33) | copy-start | bytes 1540
  291.0 230.1 %all-gather.12.cloned.1.call-start = ((), (), s32[]{:S(2)}) async-start(), calls=%async_computation.10 | async-start | bytes 3276800 | tf_op jit(solution)/shard_map/all_gather | solution.py:255
  292.5 44.8 %all-to-all-start = ((bf16[128,4,240]{0,2,1:T(8,128)(2,1)}), bf16[128,4,240]{0,2,1:T(8,128)(2,1)S(1)}, u32[]{:S(2)}, u32[]{:S(2)}) async-start(bf16[128,4,240]{0,2,1:T(8,128)(2,1)} %multiply_convert_fusion.3), calls=%async_computation | async-start | bytes 491520 | tf_op jit(solution)/shard_map/all_to_all | solution.py:167
  295.9 228.7 %all-gather.10.cloned.1.call-start = ((), (), s32[]{:S(2)}) async-start(), calls=%async_computation.9 | async-start | bytes 3276800 | tf_op jit(solution)/shard_map/all_gather | solution.py:254
  329.6 6.8 %copy-start.17 = (bf16[128,2560]{1,0:T(8,128)(2,1)S(1)}, bf16[128,2560]{1,0:T(8,128)(2,1)}, u32[]{:S(2)}) copy-start(bf16[128,2560]{1,0:T(8,128)(2,1)} %get-tuple-element.21) | copy-start | bytes 1966084
  329.6 12.9 %copy-start.19 = (bf16[128,960]{0,1:T(8,128)(2,1)S(1)}, bf16[128,960]{0,1:T(8,128)(2,1)}, u32[]{:S(2)}) copy-start(bf16[128,960]{0,1:T(8,128)(2,1)} %copy-done.18) | copy-start | bytes 737284
  332.6 90.6 %collective-permute-start.1 = (bf16[128,960]{0,1:T(8,128)(2,1)}, bf16[128,960]{0,1:T(8,128)(2,1)}, u32[]{:S(2)}, u32[]{:S(2)}) collective-permute-start(bf16[128,960]{0,1:T(8,128)(2,1)} %bitcast.50), channel_id=1, source_target_pairs={{0,3},{1,0},{2,1},{3,2},{4,7},{5,4},{6,5},{7,6},{8,11},{9,8},{10,9... | collective-permute-start | bytes 737288 | tf_op jit(solution)/shard_map/ppermute | solution.py:243
  333.0 81.3 %collective-permute-start = (bf16[128,960]{0,1:T(8,128)(2,1)}, bf16[128,960]{0,1:T(8,128)(2,1)}, u32[]{:S(2)}, u32[]{:S(2)}) collective-permute-start(bf16[128,960]{0,1:T(8,128)(2,1)} %bitcast.50), channel_id=1, source_target_pairs={{0,1},{1,2},{2,3},{3,0},{4,5},{5,6},{6,7},{7,4},{8,9},{9,10},{10,1... | collective-permute-start | bytes 737288 | tf_op jit(solution)/shard_map/ppermute | solution.py:238
  337.3 65.6 %all-to-all-start.1 = ((bf16[128,4,240]{0,2,1:T(8,128)(2,1)}), bf16[128,4,240]{0,2,1:T(8,128)(2,1)}, u32[]{:S(2)}, u32[]{:S(2)}) async-start(bf16[128,4,240]{0,2,1:T(8,128)(2,1)} %bitcast.260), calls=%async_computation.1 | async-start | bytes 491520 | tf_op jit(solution)/shard_map/all_to_all | solution.py:168
  402.9 43.2 %all-to-all-start.3 = ((bf16[128,4,640]{2,0,1:T(8,128)(2,1)}), bf16[128,4,640]{2,0,1:T(8,128)(2,1)}, u32[]{:S(2)}, u32[]{:S(2)}) async-start(bf16[128,4,640]{2,0,1:T(8,128)(2,1)} %bitcast.255), calls=%async_computation.3 | async-start | bytes 1310720 | tf_op jit(solution)/shard_map/all_to_all | solution.py:170
  414.4 26.2 %collective-permute-start.2 = (bf16[128,960]{0,1:T(8,128)(2,1)}, bf16[128,960]{0,1:T(8,128)(2,1)S(1)}, u32[]{:S(2)}, u32[]{:S(2)}) collective-permute-start(bf16[128,960]{0,1:T(8,128)(2,1)} %collective-permute-done), channel_id=1, source_target_pairs={{0,1},{1,2},{2,3},{3,0},{4,5},{5,6},{6,7},{7,4},{8,9},{9,10},{10,1... | collective-permute-start | bytes 737288 | tf_op jit(solution)/shard_map/ppermute | solution.py:238
  446.2 74.9 %all-to-all-start.2 = ((bf16[128,4,240]{0,2,1:T(8,128)(2,1)}), bf16[128,4,240]{0,2,1:T(8,128)(2,1)S(1)}, u32[]{:S(2)}, u32[]{:S(2)}) async-start(bf16[128,4,240]{0,2,1:T(8,128)(2,1)} %bitcast.72), calls=%async_computation.2 | async-start | bytes 491520 | tf_op jit(solution)/shard_map/all_to_all | solution.py:169
  467.8 122.2 %reduce-scatter.12.cloned.1.call-start = ((), (), s32[]{:S(2)}) async-start(), calls=%async_computation.12 | async-start | bytes 1382400
  521.0 87.3 %reduce-scatter.14.cloned.1.call-start = ((), (), s32[]{:S(2)}) async-start(), calls=%async_computation.13 | async-start | bytes 4147200
  541.9 5.4 copy-start.13
  541.9 5.4 copy-start.24
  541.9 5.7 copy-start.11
  541.9 5.7 copy-start.30
  547.6 41.3 %copy-start.23 = (f32[128,960]{0,1:T(8,128)S(1)}, f32[128,960]{0,1:T(8,128)}, u32[]{:S(2)}) copy-start(f32[128,960]{0,1:T(8,128)} %get-tuple-element.11) | copy-start | bytes 1474564
  547.7 41.3 %copy-start.38 = (f32[128]{0:T(128)S(1)}, f32[128]{0:T(128)}, u32[]{:S(2)}) copy-start(f32[128]{0:T(128)} %get-tuple-element.36) | copy-start | bytes 1540
  (7 other events, 5.7 us)
Sparse Core Ops, SparseCore 0:
  10.8 66.9 all-gather.5
  80.7 111.7 all-gather.7
  291.1 27.5 reduce-scatter.9
  320.1 92.6 all-gather.11
  414.2 69.5 all-gather.9
  521.1 33.7 reduce-scatter.11
  558.4 49.8 reduce-scatter.13
